TPU v7x, 256 devices: a whole 4x4x8 slice. The times are simulated.
256 devices in a mesh: rep: 4 (over x_lo, core), fsdp: 64 (over z, x_hi, y).
Axes of the slice: x: 4 (x_hi: 2, x_lo: 2; x = x_hi * 2 + x_lo), y: 4, z: 8, core: 2. Of those that a mesh axis runs over, the one named last changes fastest.
Arguments:
- tokens: bfloat16 [4096, 4096], P(('rep', 'fsdp')), may hold values from -6 to 6
- readout: bfloat16 [4096, 14336], P('rep', 'fsdp'), may hold values from -0.046875 to 0.046875
- resp_mask: int32 [4096], P('rep'), may hold values 0 or 1
- order: int32 [4, 64], P('rep'), may hold values from 0 to 63, each once within a row
- w_gate: bfloat16 [4, 14336, 4096], P('rep', 'fsdp'), may hold values from -0.09375 to 0.09375
- w_up: bfloat16 [4, 14336, 4096], P('rep', 'fsdp'), may hold values from -0.09375 to 0.09375
- outer_gate: bfloat16 [14336, 4096], P('fsdp', 'rep'), may hold values from -0.09375 to 0.09375
- outer_up: bfloat16 [14336, 4096], P('fsdp', 'rep'), may hold values from -0.09375 to 0.09375
- moment: float32 [14336, 4096], P('fsdp', 'rep'), may hold values from -0.09375 to 0.09375
Outputs:
- loss: float32 [4], P('rep')
- grad_gate: bfloat16 [4, 14336, 4096], P('rep', 'fsdp')
- grad_up: bfloat16 [4, 14336, 4096], P('rep', 'fsdp')
- new_outer: bfloat16 [14336, 4096], P('fsdp', 'rep')
- new_moment: float32 [14336, 4096], P('fsdp', 'rep')
Inputs may be any that keep to these rules, and one draw needn't show every extreme that they name: Each row of order holds every sequence number of its group once.
All inputs are finite; a program needn't handle non-finite values. Where the computation divides by a largest or mean magnitude, that divisor is 1e-20 or more. No bound on the sum of `resp_mask` on one device may be relied on, other than what follows from the above.
Results may differ from a plain program's by a relative error of at most 0.022.
Values may be sent and summed in bfloat16 or wider, within the bound.
A program may use at most 128 MiB of HBM per device.

v0:
```python
import jax
import jax.numpy as jnp
from jax import lax
from jax.sharding import PartitionSpec as P

BLOCK = 128
LEN = 16
dpo_beta = 0.1
outer_rate = 0.7
outer_mu = 0.9
tiny_eps = 1e-06


def project(rows, weight):
    return lax.dot_general(
        rows, weight, (((1,), (1,)), ((), ())), preferred_element_type=jnp.float32
    )


def local_scores(hidden, readout, mask_f, seqs):
    per_token = jnp.sum(hidden.astype(jnp.float32) * readout.astype(jnp.float32), axis=1)
    return jnp.sum((per_token * mask_f).reshape(seqs, LEN), axis=1)


def per_device(tokens, readout, resp_mask, order, w_gate, w_up, outer_gate, outer_up, moment):
    full_gate, full_up = (
        lax.all_gather(outer_gate, "rep", axis=1, tiled=True),
        lax.all_gather(outer_up, "rep", axis=1, tiled=True),
    )
    policy_gate = w_gate[0]
    policy_up = w_up[0]
    inputs = lax.all_gather(tokens, "fsdp", axis=0, tiled=True)
    gate = project(inputs, policy_gate)
    upper = project(inputs, policy_up)
    gate_ref = project(inputs, full_gate)
    upper_ref = project(inputs, full_up)
    group_tok = inputs.shape[0]
    seqs = group_tok // LEN
    mask_f = resp_mask.astype(jnp.float32)
    hidden = (jax.nn.silu(gate) * upper).astype(jnp.bfloat16)
    hidden_ref = (jax.nn.silu(gate_ref) * upper_ref).astype(jnp.bfloat16)
    score, score_ref = lax.psum(
        (
            local_scores(hidden, readout, mask_f, seqs),
            local_scores(hidden_ref, readout, mask_f, seqs),
        ),
        "fsdp",
    )
    places = jnp.arange(seqs, dtype=jnp.int32)
    pick_chosen = (order[0, 0::2][:, None] == places[None, :]).astype(jnp.float32)
    pick_rejected = (order[0, 1::2][:, None] == places[None, :]).astype(jnp.float32)
    relative = score - score_ref
    highest = lax.Precision.HIGHEST
    margin = dpo_beta * (
        jnp.dot(pick_chosen, relative, precision=highest)
        - jnp.dot(pick_rejected, relative, precision=highest)
    )
    loss = jnp.mean(jax.nn.softplus(-margin)).reshape(1)
    weight = dpo_beta * jax.nn.sigmoid(-margin) / pick_chosen.shape[0]
    coef = jnp.dot(weight, pick_rejected - pick_chosen, precision=highest)
    token_grad = jnp.broadcast_to(coef[:, None], (seqs, LEN)).reshape(-1) * mask_f
    hidden_grad = token_grad[:, None] * readout.astype(jnp.float32)
    sigma = jax.nn.sigmoid(gate)
    gate_grad = (hidden_grad * upper * sigma * (1.0 + gate * (1.0 - sigma))).astype(jnp.bfloat16)
    up_grad = (hidden_grad * jax.nn.silu(gate)).astype(jnp.bfloat16)
    contract = (((0,), (0,)), ((), ()))
    grad_gate = lax.dot_general(
        gate_grad, inputs, contract, preferred_element_type=jnp.float32
    ).astype(jnp.bfloat16)
    grad_up = lax.dot_general(up_grad, inputs, contract, preferred_element_type=jnp.float32).astype(
        jnp.bfloat16
    )
    unit_rows = full_gate.shape[0]
    delta = full_gate.astype(jnp.float32) - policy_gate.astype(jnp.float32)
    blocks = delta.reshape(unit_rows, -1, BLOCK)
    scale = (jnp.max(jnp.abs(blocks), axis=2, keepdims=True) + tiny_eps).astype(jnp.bfloat16)
    levels = (blocks / scale.astype(jnp.float32)).astype(jnp.bfloat16)
    groups = lax.axis_size("rep")
    terms = (levels.astype(jnp.float32) * scale.astype(jnp.float32)).reshape(unit_rows, -1)
    total = lax.psum_scatter(
        terms.astype(jnp.bfloat16), "rep", scatter_dimension=1, tiled=True
    ).astype(jnp.float32)
    average = total / groups
    new_moment = outer_mu * moment + average
    new_outer = (
        outer_gate.astype(jnp.float32) - outer_rate * (average + outer_mu * new_moment)
    ).astype(jnp.bfloat16)
    return (loss, grad_gate[None], grad_up[None], new_outer, new_moment)


def solution(mesh):
    return jax.shard_map(
        per_device,
        mesh=mesh,
        in_specs=(
            P(("rep", "fsdp"), None),
            P("rep", "fsdp"),
            P("rep"),
            P("rep", None),
            P("rep", "fsdp", None),
            P("rep", "fsdp", None),
            P("fsdp", "rep"),
            P("fsdp", "rep"),
            P("fsdp", "rep"),
        ),
        out_specs=(
            P("rep"),
            P("rep", "fsdp", None),
            P("rep", "fsdp", None),
            P("fsdp", "rep"),
            P("fsdp", "rep"),
        ),
        check_vma=False,
    )
```

profile of v0, /device:TPU:2, one launch (start us, length us, event | category | flops | bytes accessed | tf_op | source)
XLA Modules:
  0.0 466.0 jit_solution(16427178451897451544)
XLA Ops:
  8.1 0.7 all-gather.6.cloned.1.call-update
  8.8 32.6 %all-gather.6.cloned.1.call-done = bf16[224,4096]{1,0:T(8,128)(2,1)} async-done(((bf16[224,1024]{1,0:T(8,128)(2,1)}), bf16[224,4096]{1,0:T(8,128)(2,1)}) %all-gather.6.cloned.1.call-update) | async-done | bytes 1835024 | tf_op jit(solution)/shard_map/all_gather | solution.py:27
  41.4 2.7 abs_bitcast_fusion
  44.2 2.4 copy.14
  46.6 3.1 reduce_max.9
  49.7 1.0 div.44
  50.7 0.5 copy-done.1
  51.2 0.6 copy-done.2
  51.7 4.3 fusion.3
  56.1 0.5 all-gather.4.cloned.1.call-update
  56.7 0.2 all-gather.8.cloned.1.call-start
  56.9 0.4 all-gather.8.cloned.1.call-update
  57.5 29.5 %reduce-scatter.2.cloned.1.call-done = bf16[224,1024]{1,0:T(8,128)(2,1)} async-done(((bf16[224,4096]{1,0:T(8,128)(2,1)}), bf16[224,1024]{1,0:T(8,128)(2,1)}) %reduce-scatter.2.cloned.1.call-update) | async-done | bytes 458768 | tf_op jit(solution)/shard_map/reduce_scatter | solution.py:80
  87.0 2.4 subtract_convert_fusion
  89.4 125.4 %all-gather.4.cloned.1.call-done = bf16[1024,4096]{1,0:T(8,128)(2,1)} async-done(((bf16[16,4096]{1,0:T(8,128)(2,1)}), bf16[1024,4096]{1,0:T(8,128)(2,1)}) %all-gather.4.cloned.1.call-update) | async-done | bytes 8388624 | tf_op jit(solution)/shard_map/all_gather | solution.py:32
  214.9 7.6 %fusion.6 = f32[1024,224]{0,1:T(8,128)} fusion(bf16[1024,4096]{1,0:T(8,128)(2,1)} %all-gather.4.cloned.1.call-done, bf16[1,224,4096]{2,1,0:T(8,128)(2,1)} %param.13), kind=kOutput, calls=%fused_computation.12 | convolution fusion | flops 1879048192 | bytes 11141120 | tf_op jit(solution)/shard_map/dot_general | solution.py:15
  222.5 3.6 fusion.47
  226.1 16.0 %all-gather.8.cloned.1.call-done = bf16[224,4096]{1,0:T(8,128)(2,1)} async-done(((bf16[224,1024]{1,0:T(8,128)(2,1)}), bf16[224,4096]{1,0:T(8,128)(2,1)}) %all-gather.8.cloned.1.call-update) | async-done | bytes 1835024 | tf_op jit(solution)/shard_map/all_gather | solution.py:28
  242.1 7.1 %fusion.10 = f32[1024]{0:T(1024)S(1)} fusion(bf16[1024,224]{0,1:T(8,128)(2,1)S(1)} %copy-done.8, bf16[1024,4096]{1,0:T(8,128)(2,1)} %all-gather.4.cloned.1.call-done, bf16[224,4096]{1,0:T(8,128)(2,1)} %all-gather.8.cloned.1.call-done, f32[1024,224]{0,1:T(8,128)} %fusion.47), kind=kOutput, calls=%fused_computation.20 | convolution fusion | flops 1881340928 | bytes 11603968 | tf_op jit(solution)/shard_map/dot_general | solution.py:15
  249.2 7.1 %fusion.19 = (f32[1024]{0:T(1024)S(1)}, f32[1024,224]{0,1:T(8,128)}) fusion(bf16[1024,224]{0,1:T(8,128)(2,1)S(1)} %copy-done.8, f32[1024,224]{0,1:T(8,128)S(1)} %copy-done.10, bf16[1024,4096]{1,0:T(8,128)(2,1)} %all-gather.4.cloned.1.call-done, bf16[1,224,4096]{2,1,0:T(8,128)(2,1)S(1)} %copy-done), kind=kOutput, calls=%fused_computation.32 | convolution fusion | flops 1881340928 | bytes 12521472 | tf_op jit(solution)/shard_map/dot_general | solution.py:15
  256.7 184.5 %all-reduce = (f32[64]{0:T(128)S(1)}, f32[64]{0:T(128)S(1)}) all-reduce(f32[64]{0:T(128)S(1)} %reduce_sum.46, f32[64]{0:T(128)S(1)} %reduce_sum.48), channel_id=1, replica_groups=mesh['rep'=4,'fsdp'=64] {'fsdp'}, use_global_device_ids=true, to_apply=%region_2.3 | all-reduce | flops 128 | bytes 1024 | tf_op jit(solution)/shard_map/psum | solution.py:42
  441.4 0.8 fusion.35
  443.3 7.2 %fusion.1 = bf16[1,224,4096]{2,1,0:T(8,128)(2,1)} fusion(bf16[1024,4096]{1,0:T(8,128)(2,1)} %all-gather.4.cloned.1.call-done, bf16[1024,224]{0,1:T(8,128)(2,1)S(1)} %copy-done.8, f32[1024]{0:T(1024)S(1)} %convert_multiply_fusion.4, f32[1024,224]{0,1:T(8,128)} %fusion.6), kind=kOutput, calls=%fused_computation.3 | convolution fusion | flops 1881800704 | bytes 11603968 | tf_op jit(solution)/shard_map/dot_general | solution.py:70
  450.5 6.9 %fusion = bf16[1,224,4096]{2,1,0:T(8,128)(2,1)} fusion(bf16[1024,4096]{1,0:T(8,128)(2,1)} %all-gather.4.cloned.1.call-done, f32[1024,224]{0,1:T(8,128)S(1)} %copy-done.12, bf16[1024,224]{0,1:T(8,128)(2,1)S(1)} %copy-done.8, f32[1024,224]{0,1:T(8,128)S(1)} %copy-done.11, f32[1024]{0:T(1024)S(1)} %convert_multiply_fusion.4), kind=kOutput, calls=%fused_computation.2 | convolution fusion | flops 1882718208 | bytes 12521472 | tf_op jit(solution)/shard_map/dot_general | solution.py:67
  (41 shorter events, 1.4 us)
Async XLA Ops:
  8.0 241.2 %copy-start = (bf16[1,224,4096]{2,1,0:T(8,128)(2,1)S(1)}, bf16[1,224,4096]{2,1,0:T(8,128)(2,1)}, u32[]{:S(2)}) copy-start(bf16[1,224,4096]{2,1,0:T(8,128)(2,1)} %param.14) | copy-start | bytes 5505028
  8.0 33.4 %all-gather.6.cloned.1.call-start = ((), (), s32[]{:S(2)}) async-start(), calls=%async_computation.2 | async-start | bytes 2293760 | tf_op jit(solution)/shard_map/all_gather | solution.py:27
  8.7 78.3 %reduce-scatter.2.cloned.1.call-start = ((), (), s32[]{:S(2)}) async-start(), calls=%async_computation.4 | async-start | bytes 2293760 | tf_op jit(solution)/shard_map/reduce_scatter | solution.py:80
  49.7 1.5 copy-start.1
  49.7 2.0 copy-start.2
  51.7 5.5 %copy-start.9 = (s32[1,64]{1,0:T(1,128)S(1)}, s32[1,64]{1,0:T(1,128)}, u32[]{:S(2)}) copy-start(s32[1,64]{1,0:T(1,128)} %param.12) | copy-start | bytes 772
  51.7 35.3 %copy-start.4 = (bf16[224,1024]{1,0:T(8,128)(2,1)S(1)}, bf16[224,1024]{1,0:T(8,128)(2,1)}, u32[]{:S(2)}) copy-start(bf16[224,1024]{1,0:T(8,128)(2,1)} %param.15) | copy-start | bytes 1376260
  51.7 35.3 %copy-start.5 = (f32[224,1024]{1,0:T(8,128)S(1)}, f32[224,1024]{1,0:T(8,128)}, u32[]{:S(2)}) copy-start(f32[224,1024]{1,0:T(8,128)} %param.17) | copy-start | bytes 2752516
  56.1 158.8 %all-gather.4.cloned.1.call-start = ((), (), s32[]{:S(2)}) async-start(), calls=%async_computation.1 | async-start | bytes 8519680 | tf_op jit(solution)/shard_map/all_gather | solution.py:32
  56.7 185.4 %all-gather.8.cloned.1.call-start = ((), (), s32[]{:S(2)}) async-start(), calls=%async_computation.3 | async-start | bytes 2293760 | tf_op jit(solution)/shard_map/all_gather | solution.py:28
  214.9 7.6 %copy-start.3 = (bf16[224,4096]{1,0:T(8,128)(2,1)S(1)}, bf16[224,4096]{1,0:T(8,128)(2,1)}, u32[]{:S(2)}) copy-start(bf16[224,4096]{1,0:T(8,128)(2,1)} %all-gather.6.cloned.1.call-done) | copy-start | bytes 5505028
  214.9 7.6 %copy-start.7 = (bf16[1024,4096]{1,0:T(8,128)(2,1)S(1)}, bf16[1024,4096]{1,0:T(8,128)(2,1)}, u32[]{:S(2)}) copy-start(bf16[1024,4096]{1,0:T(8,128)(2,1)} %all-gather.4.cloned.1.call-done) | copy-start | bytes 25165828
  222.5 19.6 %copy-start.8 = (bf16[1024,224]{0,1:T(8,128)(2,1)S(1)}, bf16[1024,224]{0,1:T(8,128)(2,1)}, u32[]{:S(2)}) copy-start(bf16[1024,224]{0,1:T(8,128)(2,1)} %param.10) | copy-start | bytes 1376260
  242.1 7.1 %copy-start.10 = (f32[1024,224]{0,1:T(8,128)S(1)}, f32[1024,224]{0,1:T(8,128)}, u32[]{:S(2)}) copy-start(f32[1024,224]{0,1:T(8,128)} %fusion.6) | copy-start | bytes 2752516
  249.2 7.2 %copy-start.6 = (s32[1024]{0:T(1024)S(1)}, s32[1024]{0:T(1024)}, u32[]{:S(2)}) copy-start(s32[1024]{0:T(1024)} %param.11) | copy-start | bytes 12292
  443.3 7.2 %copy-start.11 = (f32[1024,224]{0,1:T(8,128)S(1)}, f32[1024,224]{0,1:T(8,128)}, u32[]{:S(2)}) copy-start(f32[1024,224]{0,1:T(8,128)} %fusion.6) | copy-start | bytes 2752516
  443.3 7.2 %copy-start.12 = (f32[1024,224]{0,1:T(8,128)S(1)}, f32[1024,224]{0,1:T(8,128)}, u32[]{:S(2)}) copy-start(f32[1024,224]{0,1:T(8,128)} %get-tuple-element.12) | copy-start | bytes 2752516
Sparse Core Ops, SparseCore 0:
  10.7 30.7 all-gather.5
  56.2 30.7 reduce-scatter.1
Sparse Core Ops, SparseCore 1:
  60.1 154.7 all-gather.3
  216.5 25.5 all-gather.7
where the time goes:
time: 466 us
  waiting for transfers between devices  205 us (44%)
  blocking collectives  185 us (40%)
  matrix products  40.7 us (9%)
  between operations  17.4 us (4%)
  other arithmetic  12.8 us (3%)
  local copies, waits for them, and re-layouts  5.06 us (1%)
    psum x1, blocking collectives, per_device(): lax.psum((local_scores(hidden, readout, mask_f, seqs), local_scores(hidde...  185 us
    all_gather x1, waiting for transfers between devices, per_device(): inputs = lax.all_gather(tokens, 'fsdp', axis=0, tiled=True)  125 us
    all_gather x1, waiting for transfers between devices, per_device(): lax.all_gather(outer_gate, 'rep', axis=1, tiled=True)  32.6 us
    reduce_scatter x1, waiting for transfers between devices, per_device(): lax.psum_scatter(terms.astype(jnp.bfloat16), 'rep', scatter_dimension=1,...  29.5 us
    dot_general x4, matrix products, project(): lax.dot_general(rows, weight, (((1,), (1,)), ((), ())), preferred_element...  25.4 us
    all_gather x1, waiting for transfers between devices, per_device(): lax.all_gather(outer_up, 'rep', axis=1, tiled=True)  16 us
  transfers between devices with their start and end apart: 4, of which 4 were waited for; matrix products, arithmetic and copies ran while one was open for 3% of the time, Pallas kernels for 0%

commit v1 on v0

--- a/solution.py
+++ b/solution.py
@@ -29,7 +29,9 @@
     )
     policy_gate = w_gate[0]
     policy_up = w_up[0]
-    inputs = lax.all_gather(tokens, "fsdp", axis=0, tiled=True)
+    inputs = jnp.concatenate(
+        lax.all_to_all(jnp.stack([tokens] * lax.axis_size("fsdp")), "fsdp", 0, 0), axis=0
+    )
     gate = project(inputs, policy_gate)
     upper = project(inputs, policy_up)
     gate_ref = project(inputs, full_gate)

time: 466 us -> 447 us (0.959)
  waiting for transfers between devices: 205 us -> 167 us
  starting transfers between devices: 0.34 us -> 14.2 us
  local copies, waits for them, and re-layouts: 5.06 us -> 10.4 us
    all_gather x1 -> x0, waiting for transfers between devices: 125 us -> none  [per_device(): inputs = lax.all_gather(tokens, 'fsdp', axis=0, tiled=True)]
    all_to_all x0 -> x1, waiting for transfers between devices: none -> 64.6 us  [per_device(): lax.all_to_all(jnp.stack([tokens] * lax.axis_size('fsdp')), 'fsdp', 0, 0)]
    reduce_scatter x1, waiting for transfers between devices: 29.5 us -> 51.1 us  [per_device(): lax.psum_scatter(terms.astype(jnp.bfloat16), 'rep', scatter_dimension=1,...]
    all_gather x1, waiting for transfers between devices: 32.6 us -> 50.6 us  [per_device(): lax.all_gather(outer_gate, 'rep', axis=1, tiled=True)]
    all_gather x1, waiting for transfers between devices: 16 us -> 0.01 us  [per_device(): lax.all_gather(outer_up, 'rep', axis=1, tiled=True)]
    all_to_all x0 -> x1, starting transfers between devices: none -> 13.9 us  [per_device(): lax.all_to_all(jnp.stack([tokens] * lax.axis_size('fsdp')), 'fsdp', 0, 0)]
    another operation x0 -> x1, local copies, waits for them, and re-layouts: none -> 5.3 us  [per_device(): jnp.stack([tokens] * lax.axis_size('fsdp'))]
  transfers between devices with their start and end apart: 4 -> 4, of which waited for: 4 -> 3; matrix products, arithmetic and copies ran while one was open for 3% -> 8% of each run, Pallas kernels for 0% -> 0%
where the time goes in v1:
time: 447 us; the launch traced here: 446 us
  blocking collectives  183 us (41%)
  waiting for transfers between devices  167 us (37%)
  matrix products  43.4 us (10%)
  between operations  15.7 us (4%)
  starting transfers between devices  14.2 us (3%)
  other arithmetic  12.8 us (3%)
  local copies, waits for them, and re-layouts  10.4 us (2%)
    psum x1, blocking collectives, per_device(): lax.psum((local_scores(hidden, readout, mask_f, seqs), local_scores(hidde...  183 us
    all_to_all x1, waiting for transfers between devices, per_device(): lax.all_to_all(jnp.stack([tokens] * lax.axis_size('fsdp')), 'fsdp', 0, 0)  64.6 us
    reduce_scatter x1, waiting for transfers between devices, per_device(): lax.psum_scatter(terms.astype(jnp.bfloat16), 'rep', scatter_dimension=1,...  51.1 us
    all_gather x1, waiting for transfers between devices, per_device(): lax.all_gather(outer_gate, 'rep', axis=1, tiled=True)  50.6 us
    dot_general x4, matrix products, project(): lax.dot_general(rows, weight, (((1,), (1,)), ((), ())), preferred_element...  28.1 us
    all_to_all x1, starting transfers between devices, per_device(): lax.all_to_all(jnp.stack([tokens] * lax.axis_size('fsdp')), 'fsdp', 0, 0)  13.9 us
  transfers between devices with their start and end apart: 4, of which 3 were waited for; matrix products, arithmetic and copies ran while one was open for 8% of the time, Pallas kernels for 0%

profile of v1, /device:TPU:2, one launch (start us, length us, event | category | flops | bytes accessed | tf_op | source)
XLA Modules:
  0.0 446.5 jit_solution(10966070103536224100)
XLA Ops:
  7.2 5.3 %stack.2 = bf16[64,16,4096]{2,1,0:T(8,128)(2,1)} broadcast(bf16[16,4096]{1,0:T(8,128)(2,1)} %param.9), dimensions={1,2} | broadcast | bytes 8519680 | tf_op jit(solution)/shard_map/stack | solution.py:33
  12.5 13.9 %all-to-all-start = ((bf16[64,16,4096]{2,1,0:T(8,128)(2,1)}), bf16[64,16,4096]{2,1,0:T(8,128)(2,1)}, u32[]{:S(2)}, u32[]{:S(2)}) async-start(bf16[64,16,4096]{2,1,0:T(8,128)(2,1)} %stack.2), calls=%async_computation | async-start | bytes 16777216 | tf_op jit(solution)/shard_map/all_to_all | solution.py:33
  26.5 0.7 all-gather.3.cloned.1.call-update
  27.2 50.6 %all-gather.3.cloned.1.call-done = bf16[224,4096]{1,0:T(8,128)(2,1)} async-done(((bf16[224,1024]{1,0:T(8,128)(2,1)}), bf16[224,4096]{1,0:T(8,128)(2,1)}) %all-gather.3.cloned.1.call-update) | async-done | bytes 1835024 | tf_op jit(solution)/shard_map/all_gather | solution.py:27
  77.8 2.7 abs_bitcast_fusion
  80.5 2.4 copy.14
  82.9 3.1 reduce_max.9
  86.1 1.0 div.44
  87.1 0.5 copy-done.1
  87.5 0.6 copy-done.2
  88.1 4.3 fusion.3
  92.4 0.2 all-gather.5.cloned.1.call-start
  92.7 0.5 all-gather.5.cloned.1.call-update
  93.4 51.1 %reduce-scatter.2.cloned.1.call-done = bf16[224,1024]{1,0:T(8,128)(2,1)} async-done(((bf16[224,4096]{1,0:T(8,128)(2,1)}), bf16[224,1024]{1,0:T(8,128)(2,1)}) %reduce-scatter.2.cloned.1.call-update) | async-done | bytes 458768 | tf_op jit(solution)/shard_map/reduce_scatter | solution.py:82
  144.6 2.4 subtract_convert_fusion
  146.9 64.6 %all-to-all-done = bf16[64,16,4096]{2,1,0:T(8,128)(2,1)} async-done(((bf16[64,16,4096]{2,1,0:T(8,128)(2,1)}), bf16[64,16,4096]{2,1,0:T(8,128)(2,1)}, u32[]{:S(2)}, u32[]{:S(2)}) %all-to-all-start) | async-done | bytes 8388640 | tf_op jit(solution)/shard_map/all_to_all | solution.py:33
  211.5 6.7 %fusion.6 = f32[1024,224]{0,1:T(8,128)S(1)} fusion(bf16[1024,4096]{1,0:T(8,128)(2,1)} %bitcast.1, bf16[1,224,4096]{2,1,0:T(8,128)(2,1)} %param.13), kind=kOutput, calls=%fused_computation.12 | convolution fusion | flops 1879048192 | bytes 11141120 | tf_op jit(solution)/shard_map/dot_general | solution.py:15
  218.2 7.4 %fusion.47 = f32[1024,224]{0,1:T(8,128)} fusion(bf16[1024,4096]{1,0:T(8,128)(2,1)} %bitcast.1, bf16[224,4096]{1,0:T(8,128)(2,1)S(1)} %copy-done.3), kind=kOutput, calls=%fused_computation.70 | convolution fusion | flops 1879048192 | bytes 11141120 | tf_op jit(solution)/shard_map/dot_general | solution.py:15
  225.6 7.0 %fusion.19 = (f32[1024]{0:T(1024)S(1)}, f32[1024,224]{0,1:T(8,128)}) fusion(bf16[1024,224]{0,1:T(8,128)(2,1)S(1)} %copy-done.7, f32[1024,224]{0,1:T(8,128)S(1)} %fusion.6, bf16[1024,4096]{1,0:T(8,128)(2,1)} %bitcast.1, bf16[1,224,4096]{2,1,0:T(8,128)(2,1)S(1)} %copy-done), kind=kOutput, calls=%fused_computation.32 | convolution fusion | flops 1881340928 | bytes 12521472 | tf_op jit(solution)/shard_map/dot_general | solution.py:15
  232.7 7.0 %fusion.10 = f32[1024]{0:T(1024)S(1)} fusion(bf16[1024,224]{0,1:T(8,128)(2,1)S(1)} %copy-done.7, bf16[1024,4096]{1,0:T(8,128)(2,1)} %bitcast.1, bf16[224,4096]{1,0:T(8,128)(2,1)} %all-gather.5.cloned.1.call-done, f32[1024,224]{0,1:T(8,128)} %fusion.47), kind=kOutput, calls=%fused_computation.20 | convolution fusion | flops 1881340928 | bytes 11603968 | tf_op jit(solution)/shard_map/dot_general | solution.py:15
  240.1 182.6 %all-reduce = (f32[64]{0:T(128)S(1)}, f32[64]{0:T(128)S(1)}) all-reduce(f32[64]{0:T(128)S(1)} %reduce_sum.46, f32[64]{0:T(128)S(1)} %reduce_sum.48), channel_id=1, replica_groups=mesh['rep'=4,'fsdp'=64] {'fsdp'}, use_global_device_ids=true, to_apply=%region_2.3 | all-reduce | flops 128 | bytes 1024 | tf_op jit(solution)/shard_map/psum | solution.py:44
  422.9 0.8 fusion.35
  424.1 7.2 %fusion.1 = bf16[1,224,4096]{2,1,0:T(8,128)(2,1)} fusion(bf16[1024,4096]{1,0:T(8,128)(2,1)} %bitcast.1, bf16[1024,224]{0,1:T(8,128)(2,1)S(1)} %copy-done.7, f32[1024]{0:T(1024)S(1)} %convert_multiply_fusion.4, f32[1024,224]{0,1:T(8,128)} %copy-done.9), kind=kOutput, calls=%fused_computation.3 | convolution fusion | flops 1881800704 | bytes 11603968 | tf_op jit(solution)/shard_map/dot_general | solution.py:72
  431.3 6.9 %fusion = bf16[1,224,4096]{2,1,0:T(8,128)(2,1)} fusion(bf16[1024,4096]{1,0:T(8,128)(2,1)} %bitcast.1, f32[1024,224]{0,1:T(8,128)S(1)} %copy-done.11, bf16[1024,224]{0,1:T(8,128)(2,1)S(1)} %copy-done.7, f32[1024,224]{0,1:T(8,128)S(1)} %copy-done.10, f32[1024]{0:T(1024)S(1)} %convert_multiply_fusion.4), kind=kOutput, calls=%fused_computation.2 | convolution fusion | flops 1882718208 | bytes 12521472 | tf_op jit(solution)/shard_map/dot_general | solution.py:69
  (39 shorter events, 1.3 us)
Async XLA Ops:
  7.2 218.5 %copy-start = (bf16[1,224,4096]{2,1,0:T(8,128)(2,1)S(1)}, bf16[1,224,4096]{2,1,0:T(8,128)(2,1)}, u32[]{:S(2)}) copy-start(bf16[1,224,4096]{2,1,0:T(8,128)(2,1)} %param.14) | copy-start | bytes 5505028
  12.5 199.0 %all-to-all-start = ((bf16[64,16,4096]{2,1,0:T(8,128)(2,1)}), bf16[64,16,4096]{2,1,0:T(8,128)(2,1)}, u32[]{:S(2)}, u32[]{:S(2)}) async-start(bf16[64,16,4096]{2,1,0:T(8,128)(2,1)} %stack.2), calls=%async_computation | async-start | bytes 16777216 | tf_op jit(solution)/shard_map/all_to_all | solution.py:33
  26.4 51.4 %all-gather.3.cloned.1.call-start = ((), (), s32[]{:S(2)}) async-start(), calls=%async_computation.2 | async-start | bytes 2293760 | tf_op jit(solution)/shard_map/all_gather | solution.py:27
  27.2 117.4 %reduce-scatter.2.cloned.1.call-start = ((), (), s32[]{:S(2)}) async-start(), calls=%async_computation.4 | async-start | bytes 2293760 | tf_op jit(solution)/shard_map/reduce_scatter | solution.py:82
  86.0 1.5 copy-start.1
  86.0 2.0 copy-start.2
  88.1 5.1 %copy-start.8 = (s32[1,64]{1,0:T(1,128)S(1)}, s32[1,64]{1,0:T(1,128)}, u32[]{:S(2)}) copy-start(s32[1,64]{1,0:T(1,128)} %param.12) | copy-start | bytes 772
  88.1 56.5 %copy-start.4 = (bf16[224,1024]{1,0:T(8,128)(2,1)S(1)}, bf16[224,1024]{1,0:T(8,128)(2,1)}, u32[]{:S(2)}) copy-start(bf16[224,1024]{1,0:T(8,128)(2,1)} %param.15) | copy-start | bytes 1376260
  88.1 56.5 %copy-start.5 = (f32[224,1024]{1,0:T(8,128)S(1)}, f32[224,1024]{1,0:T(8,128)}, u32[]{:S(2)}) copy-start(f32[224,1024]{1,0:T(8,128)} %param.17) | copy-start | bytes 2752516
  92.4 140.2 %all-gather.5.cloned.1.call-start = ((), (), s32[]{:S(2)}) async-start(), calls=%async_computation.3 | async-start | bytes 2293760 | tf_op jit(solution)/shard_map/all_gather | solution.py:28
  211.5 6.7 %copy-start.3 = (bf16[224,4096]{1,0:T(8,128)(2,1)S(1)}, bf16[224,4096]{1,0:T(8,128)(2,1)}, u32[]{:S(2)}) copy-start(bf16[224,4096]{1,0:T(8,128)(2,1)} %all-gather.3.cloned.1.call-done) | copy-start | bytes 5505028
  218.2 7.4 %copy-start.9 = (f32[1024,224]{0,1:T(8,128)}, f32[1024,224]{0,1:T(8,128)S(1)}, u32[]{:S(2)}) copy-start(f32[1024,224]{0,1:T(8,128)S(1)} %fusion.6) | copy-start | bytes 2752516
  218.2 7.4 %copy-start.7 = (bf16[1024,224]{0,1:T(8,128)(2,1)S(1)}, bf16[1024,224]{0,1:T(8,128)(2,1)}, u32[]{:S(2)}) copy-start(bf16[1024,224]{0,1:T(8,128)(2,1)} %param.10) | copy-start | bytes 1376260
  232.7 7.0 %copy-start.6 = (s32[1024]{0:T(1024)S(1)}, s32[1024]{0:T(1024)}, u32[]{:S(2)}) copy-start(s32[1024]{0:T(1024)} %param.11) | copy-start | bytes 12292
  424.1 7.2 %copy-start.10 = (f32[1024,224]{0,1:T(8,128)S(1)}, f32[1024,224]{0,1:T(8,128)}, u32[]{:S(2)}) copy-start(f32[1024,224]{0,1:T(8,128)} %copy-done.9) | copy-start | bytes 2752516
  424.1 7.2 %copy-start.11 = (f32[1024,224]{0,1:T(8,128)S(1)}, f32[1024,224]{0,1:T(8,128)}, u32[]{:S(2)}) copy-start(f32[1024,224]{0,1:T(8,128)} %get-tuple-element.12) | copy-start | bytes 2752516
Sparse Core Ops, SparseCore 0:
  29.1 48.6 all-gather.2
  92.6 51.9 reduce-scatter.1
  146.4 48.6 all-gather.4
